TPU v7x, 512 devices: a whole 4x8x8 slice. The times are simulated.
512 devices in a mesh: wide: 64 (over y, z_lo, core), narrow: 8 (over x, z_hi).
Axes of the slice: x: 4, y: 8, z: 8 (z_hi: 2, z_lo: 4; z = z_hi * 4 + z_lo), core: 2. Of those that a mesh axis runs over, the one named last changes fastest.
Arguments:
- loads: float32 [2048, 24, 128], P(('wide', 'narrow')), may hold values from -6 to 6
- diagonal: float32 [2048, 128], P(('wide', 'narrow')), may hold values from 2 to 7
- stiffness: float32 [2048, 4, 128, 128], P(('wide', 'narrow')), may hold values from 0 to 0.001953125
- neighbors: int32 [2048, 4], P(('wide', 'narrow')), may hold values from 0 to 7
- slot_mask: int32 [2048, 4], P(('wide', 'narrow')), may hold values 0 or 1
- send_list: int32 [2048], P(('wide', 'narrow')), may hold values from 0 to 3
- aggregate: int32 [2048, 128], P(('wide', 'narrow')), may hold values from 0 to 127
- coarse_inverse: float32 [8192, 8192], P(('wide', 'narrow')), may hold values from -0.0078125 to 0.0078125
Outputs:
- correction: float32 [2048, 24, 128], P(('wide', 'narrow'))
- residual: float32 [2048, 24, 128], P(('wide', 'narrow'))
Inputs may be any that keep to these rules, and one draw needn't show every extreme that they name: `neighbors`: indices into the extended list of the block's group. `send_list`: block indices within the sending group. aggregate indices among the 128 aggregates of the particle's wide coordinate.
All inputs are finite; a program needn't handle non-finite values. No bound on the sum of `slot_mask` on one device may be relied on, other than what follows from the above.
Results may differ from a plain program's by a relative error of at most 0.00025.
Values sent between devices are 32-bit elements; how exact they have to be, the bound alone decides.
A program may use at most 64 MiB of HBM per device.

v0:
```python
import jax
import jax.numpy as jnp
from jax import lax
from jax.sharding import PartitionSpec as P

SWEEPS = 2


highest = lax.Precision.HIGHEST


def with_halo(block, sides, width):
    for axis, dim in sides:
        count = lax.axis_size(axis)
        forward = [(i, i + 1) for i in range(count - 1)]
        backward = [(target, source) for source, target in forward]
        low = lax.ppermute(
            lax.slice_in_dim(block, block.shape[dim] - width, None, axis=dim), axis, forward
        )
        high = lax.ppermute(lax.slice_in_dim(block, 0, width, axis=dim), axis, backward)
        block = jnp.concatenate([low, block, high], axis=dim)
    return block


def shards(loads, diagonal, stiffness, neighbors, slot_mask, send_list, aggregate, coarse_inverse):
    ghost_rows = send_list.shape[0] // 2
    live_slots = slot_mask.astype(jnp.float32)
    diag_rows = diagonal[:, None, :]

    def operate(vector):
        outgoing = jnp.take(vector, send_list, axis=0)
        padded = with_halo(outgoing, (("wide", 0),), ghost_rows)
        extended = jnp.concatenate([vector, padded[:ghost_rows], padded[3 * ghost_rows :]], axis=0)
        gathered = jnp.take(extended, neighbors, axis=0) * live_slots[:, :, None, None]
        coupled = jnp.einsum("bscj,bsij->bci", gathered, stiffness, precision=highest)
        return diag_rows * vector - coupled

    scaled = loads / diag_rows
    row_sums = jnp.sum(jnp.sum(jnp.abs(stiffness), axis=3) * live_slots[:, :, None], axis=1)
    local_peak = jnp.max(row_sums / diagonal)
    upper_bound = 1.0 + lax.pmax(local_peak, ("wide", "narrow"))
    centre = 0.625 * upper_bound
    direction = scaled / centre
    applied = operate(direction)
    half_span = 0.375 * upper_bound
    spread_ratio = 5.0 / 3.0
    weight_prev = 0.6
    solution = direction
    remainder = loads
    for sweep_index in range(SWEEPS):
        if sweep_index > 0:
            applied = operate(direction)
        remainder = remainder - applied
        weight_now = 1.0 / (2.0 * spread_ratio - weight_prev)
        direction = (
            weight_now * weight_prev * direction
            + 2.0 * weight_now / half_span * remainder / diag_rows
        )
        solution = solution + direction
        weight_prev = weight_now
    residual = remainder - operate(direction)
    agg_cols = coarse_inverse.shape[0] * lax.axis_size("narrow")
    one_hot = (
        aggregate[:, :, None] == jnp.arange(agg_cols, dtype=jnp.int32)[None, None, :]
    ).astype(jnp.float32)
    part_sums = jnp.einsum("bci,big->cg", residual, one_hot, precision=highest)
    owned_sums = lax.psum_scatter(part_sums, "narrow", scatter_dimension=1, tiled=True)
    coarse_own = jnp.einsum(
        "ch,kh->ck",
        lax.all_gather(owned_sums, ("wide", "narrow"), axis=1, tiled=True),
        coarse_inverse,
        precision=highest,
    )
    coarse_group = lax.all_gather(coarse_own, "narrow", axis=1, tiled=True)
    spread_back = jnp.einsum("cg,big->bci", coarse_group, one_hot, precision=highest)
    return (solution + spread_back, residual)


def solution(mesh):
    return jax.shard_map(
        shards,
        mesh=mesh,
        in_specs=(
            P(("wide", "narrow"), None, None),
            P(("wide", "narrow"), None),
            P(("wide", "narrow"), None, None, None),
            P(("wide", "narrow"), None),
            P(("wide", "narrow"), None),
            P(("wide", "narrow")),
            P(("wide", "narrow"), None),
            P(("wide", "narrow"), None),
        ),
        out_specs=(P(("wide", "narrow"), None, None), P(("wide", "narrow"), None, None)),
        check_vma=False,
    )
```

profile of v0, /device:TPU:1, one launch (start us, length us, event | category | flops | bytes accessed | tf_op | source)
XLA Modules:
  0.0 1643.6 jit_solution(16821099746210735129)
XLA Ops:
  7.3 0.8 compare_and_fusion.1
  9.4 1.6 abs_reduce_fusion
  11.0 1.3 divide_reduce_fusion
  12.3 106.1 %pmax.7 = f32[]{:T(128)} all-reduce(f32[]{:T(128)} %divide_reduce_fusion), channel_id=1, replica_groups=mesh['wide'=64,'narrow'=8] {'wide','narrow'}, use_global_device_ids=true, to_apply=%region_3.0 | all-reduce | flops 1 | bytes 8 | tf_op jit(solution)/shard_map/pmax | solution.py:41
  119.7 0.8 broadcast_divide_fusion
  121.2 2.3 collective-permute-start
  123.6 2.0 collective-permute-start.1
  125.5 0.7 compare_and_fusion
  127.1 1.6 collective-permute-done.1
  129.3 2.3 divide_add_fusion.1
  132.2 2.0 collective-permute-start.2
  134.2 2.4 collective-permute-start.3
  136.6 2.7 collective-permute-done.3
  139.9 1.0 divide_add_fusion
  141.6 1.9 collective-permute-start.4
  143.5 2.4 collective-permute-start.5
  145.9 2.7 collective-permute-done.5
  149.3 1.0 fusion.6
  150.3 1.1 convolution_bitcast_fusion
  151.4 92.9 %reduce-scatter.4.cloned.1.call-done = f32[16,24]{1,0:T(8,128)} async-done(((f32[128,24]{1,0:T(8,128)}), f32[16,24]{1,0:T(8,128)}) %reduce-scatter.4.cloned.1.call-update) | async-done | bytes 1552
  244.3 1351.4 %all_gather.6 = f32[24,8192]{0,1:T(8,128)S(1)} all-gather(f32[24,16]{0,1:T(8,128)} %bitcast.46), channel_id=1, replica_groups=mesh['wide'=64,'narrow'=8] {'wide','narrow'}, dimensions={1}, use_global_device_ids=true | all-gather | bytes 787968 | tf_op jit(solution)/shard_map/all_gather | solution.py:70
  1595.7 2.4 fusion.25
  1598.1 37.6 %all_gather.7 = f32[24,128]{0,1:T(8,128)S(1)} all-gather(f32[24,16]{0,1:T(8,128)S(1)} %fusion.25), channel_id=1, replica_groups=mesh['wide'=64,'narrow'=8] {'narrow'}, dimensions={1}, use_global_device_ids=true | all-gather | bytes 13824 | tf_op jit(solution)/shard_map/all_gather | solution.py:74
  1635.8 1.0 fusion
  (40 shorter events, 6.6 us)
Async XLA Ops:
  7.2 1588.6 %copy-start = (f32[16,8192]{1,0:T(8,128)S(1)}, f32[16,8192]{1,0:T(8,128)}, u32[]{:S(2)}) copy-start(f32[16,8192]{1,0:T(8,128)} %param.19) | copy-start | bytes 1572868
  7.2 132.7 %copy-start.1 = (f32[4,4,128,128]{3,2,1,0:T(8,128)S(1)}, f32[4,4,128,128]{3,2,1,0:T(8,128)}, u32[]{:S(2)}) copy-start(f32[4,4,128,128]{3,2,1,0:T(8,128)} %param.14) | copy-start | bytes 3145732
  7.2 132.7 %copy-start.3 = (f32[4,128]{1,0:T(4,128)S(1)}, f32[4,128]{1,0:T(4,128)}, u32[]{:S(2)}) copy-start(f32[4,128]{1,0:T(4,128)} %param.13) | copy-start | bytes 6148
  7.2 143.1 %copy-start.5 = (s32[4,128]{1,0:T(4,128)S(1)}, s32[4,128]{1,0:T(4,128)}, u32[]{:S(2)}) copy-start(s32[4,128]{1,0:T(4,128)} %param.18) | copy-start | bytes 6148
  7.2 237.1 %reduce-scatter.4.cloned.1.call-start = ((), (), s32[]{:S(2)}) async-start(), calls=%async_computation.1 | async-start | bytes 73728
  121.2 5.9 collective-permute-start
  123.6 5.1 collective-permute-start.1
  132.2 4.4 collective-permute-start.2
  134.2 5.1 collective-permute-start.3
  141.6 4.3 collective-permute-start.4
  143.5 5.1 collective-permute-start.5
  150.3 1447.9 %copy-start.4 = (f32[4,24,128]{2,1,0:T(8,128)}, f32[4,24,128]{2,1,0:T(8,128)S(1)}, u32[]{:S(2)}) copy-start(f32[4,24,128]{2,1,0:T(8,128)S(1)} %fusion.6) | copy-start | bytes 147460
  244.3 1391.4 %copy-start.2 = (f32[4,24,128]{2,1,0:T(8,128)S(1)}, f32[4,24,128]{2,1,0:T(8,128)}, u32[]{:S(2)}) copy-start(f32[4,24,128]{2,1,0:T(8,128)} %param.12) | copy-start | bytes 147460
Sparse Core Ops, SparseCore 0:
  151.6 92.7 reduce-scatter.3
where the time goes:
time: 1650 us; the launch traced here: 1640 us
  blocking collectives  1500 us (91%)
  waiting for transfers between devices  100 us (6%)
    all_gather x1, blocking collectives, shards(): lax.all_gather(owned_sums, ('wide', 'narrow'), axis=1, tiled=True)  1350 us
    pmax x1, blocking collectives, shards(): upper_bound = 1.0 + lax.pmax(local_peak, ('wide', 'narrow'))  106 us
    unnamed x2, waiting for transfers between devices  92.9 us
    all_gather x1, blocking collectives, shards(): coarse_group = lax.all_gather(coarse_own, 'narrow', axis=1, tiled=True)  37.6 us
  transfers between devices with their start and end apart: 7, of which 4 were waited for; matrix products, arithmetic and copies ran while one was open for 0% of the time, Pallas kernels for 0%

commit v1 on v0

v1 whole, which is shorter than its diff:
```python
import jax
import jax.numpy as jnp
from jax import lax
from jax.experimental import pallas as pl
from jax.experimental.pallas import tpu as pltpu
from jax.sharding import PartitionSpec as P

F32 = jnp.float32
BF16 = jnp.bfloat16
MESH = pl.DeviceIdType.MESH
NB, NS, VEC, BS = 4, 4, 24, 128
NX, NY, NZL, NZH = 4, 8, 4, 2
NZ = NZL * NZH
NQ = 2 * NX
N_WIDE = NY * NZL * 2
SWEEPS = 2
ROWS = 16
NT = (((1,), (1,)), ((), ()))
NN = (((1,), (0,)), ((), ()))


def split(value):
    high = value.astype(BF16).astype(F32)
    return jnp.concatenate([high, value - high], axis=0).astype(BF16)


def dot(a, b, dims):
    return lax.dot_general(a, b, dims, preferred_element_type=F32)


def folded(full):
    half = full.shape[0] // 2
    cols = full.shape[1] // 2
    return full[:half, :cols] + (full[:half, cols:] + full[half:, :cols])


def kernel(nbr, msk, snd, loads_h, diag_h, stiff_h, agg_h, inv_h, corr_h, res_h,
           loads_v, diag_v, stiff_v, agg_v, inv_v, own, ksum, sbuf, ghost, exts, w2,
           mx, inv_s, inv_r, wc, oh, ohs, p_s, a_r, b_r, c_r, d_r, e_r, res_v, corr_v,
           lsem, halo_ss, halo_rs, mx_ss, mx_rs, inv_ss, inv_rs, a_ss, a_rs, b_ss, b_rs,
           c_ss, c_rs, d_ss, d_rs, e_ss, e_rs):
    w = lax.axis_index("wide")
    n = lax.axis_index("narrow")
    core = w % 2
    zl = (w // 2) % NZL
    y = w // (2 * NZL)
    x = n // NZH
    zh = n % NZH
    z = zh * NZL + zl
    q = 2 * x + core

    def at(y_, zl_, core_, x_, zh_):
        return ((y_ * NZL + zl_) * 2 + core_, x_ * NZH + zh_)

    def xk_peer(d):
        other = (q + d) % NQ
        return at(y, zl, other % 2, other // 2, zh)

    def z_peer(d):
        other = (z + d) % NZ
        return at(y, other % NZL, core, x, other // NZL)

    def y_peer(d):
        return at((y + d) % NY, zl, core, x, zh)

    def rcopy(src, dst, ss, rs, dev):
        return pltpu.make_async_remote_copy(src_ref=src, dst_ref=dst, send_sem=ss, recv_sem=rs,
                                            device_id=dev, device_id_type=MESH)

    barrier = pltpu.get_barrier_semaphore()

    def greet(dev):
        pl.semaphore_signal(barrier, inc=1, device_id=dev, device_id_type=MESH)

    left_far = jnp.logical_and(core == 0, w > 0)
    right_far = jnp.logical_and(core == 1, w < N_WIDE - 1)
    pl.when(left_far)(lambda: greet((w - 1, n)))
    pl.when(right_far)(lambda: greet((w + 1, n)))
    for d in range(1, 8):
        greet(xk_peer(d))
        greet(z_peer(d))
        greet(y_peer(d))

    cp_loads = pltpu.make_async_copy(loads_h, loads_v, lsem.at[0])
    cp_diag = pltpu.make_async_copy(diag_h, diag_v, lsem.at[1])
    cp_stiff = [pltpu.make_async_copy(stiff_h.at[b], stiff_v.at[b], lsem.at[2 + b]) for b in range(NB)]
    cp_inv = pltpu.make_async_copy(inv_h, inv_v, lsem.at[6])
    cp_agg = pltpu.make_async_copy(agg_h, agg_v, lsem.at[7])
    for cp in [cp_loads, cp_diag] + cp_stiff + [cp_inv, cp_agg]:
        cp.start()

    @pl.when(w == 0)
    def _():
        ghost[:, 0:2] = jnp.zeros((3, 2, VEC, BS), F32)

    @pl.when(w == N_WIDE - 1)
    def _():
        ghost[:, 2:4] = jnp.zeros((3, 2, VEC, BS), F32)

    cp_loads.wait()
    cp_diag.wait()
    rdiag = [1.0 / diag_v[b:b + 1, :] for b in range(NB)]
    for b in range(NB):
        own[0, b] = loads_v[b] * rdiag[b]

    def to_left(k):
        return rcopy(sbuf.at[k, pl.ds(0, 2)], ghost.at[k, pl.ds(2, 2)], halo_ss.at[k, 0], halo_rs.at[k, 0], (w - 1, n))

    def to_right(k):
        return rcopy(sbuf.at[k, pl.ds(2, 2)], ghost.at[k, pl.ds(0, 2)], halo_ss.at[k, 1], halo_rs.at[k, 1], (w + 1, n))

    def send_halo(k):
        for j in range(4):
            sbuf[k, j] = own[k, snd[j]]
        pl.when(w > 0)(lambda: to_left(k).start())
        pl.when(w < N_WIDE - 1)(lambda: to_right(k).start())

    def wait_halo(k):
        pl.when(w < N_WIDE - 1)(lambda: to_left(k).wait_recv())
        pl.when(w > 0)(lambda: to_right(k).wait_recv())

    @pl.when(jnp.logical_or(left_far, right_far))
    def _():
        pl.semaphore_wait(barrier, 22)

    @pl.when(jnp.logical_not(jnp.logical_or(left_far, right_far)))
    def _():
        pl.semaphore_wait(barrier, 21)

    send_halo(0)

    ones = jnp.ones((8, BS), F32)
    peak = None
    for b in range(NB):
        cp_stiff[b].wait()
        total = None
        for s in range(NS):
            block = stiff_v[b, s] * msk[b, s].astype(F32)
            size = jnp.abs(block)
            total = size if total is None else total + size
            high = block.astype(BF16)
            w2[b, 0:BS, s * BS:(s + 1) * BS] = high
            w2[b, BS:2 * BS, s * BS:(s + 1) * BS] = (block - high.astype(F32)).astype(BF16)
        sums = lax.dot_general(ones, total, NT, precision=lax.Precision.HIGHEST, preferred_element_type=F32)
        ratio = sums / diag_v[b:b + 1, :]
        peak = ratio if peak is None else jnp.maximum(peak, ratio)
    mx[0, 0] = jnp.broadcast_to(jnp.max(peak, axis=1, keepdims=True), (8, BS))

    def peak_copy(stage, d):
        dev = (xk_peer, z_peer, y_peer)[stage](d)
        return rcopy(mx.at[stage, 0], mx.at[stage, d], mx_ss.at[stage, d], mx_rs.at[stage, d], dev)

    def send_peak(stage):
        for d in range(1, 8):
            peak_copy(stage, d).start()

    def take_peak(stage):
        for d in range(1, 8):
            peak_copy(stage, d).wait_recv()
        top = mx[stage, 0]
        for d in range(1, 8):
            top = jnp.maximum(top, mx[stage, d])
        return top

    send_peak(0)

    def split_own(k):
        for b in range(NB):
            exts[b] = split(own[k, b])

    split_own(0)

    cp_inv.wait()
    for j in range(NQ):
        for i in range(NY):
            col = (NQ * i + j) * BS
            inv_s[j, i] = inv_v[:, col:col + BS]

    def inv_copy(d):
        other = (q + d) % NQ
        return rcopy(inv_s.at[other], inv_r.at[q], inv_ss.at[d], inv_rs.at[d], xk_peer(d))

    for d in range(1, NQ):
        inv_copy(d).start()
    inv_r[q] = inv_s[q]

    def couple(k):
        wait_halo(k)
        for j in range(4):
            exts[NB + j] = split(ghost[k, j])
        for b in range(NB):
            fields = jnp.concatenate([exts[nbr[b, s]] for s in range(NS)], axis=1)
            coupled = folded(dot(fields, w2[b], NT))
            ksum[k, b] = coupled
            if k < SWEEPS:
                own[k + 1, b] = coupled * rdiag[b]
        if k < SWEEPS:
            send_halo(k + 1)

    couple(0)
    mx[1, 0] = take_peak(0)
    send_peak(1)
    split_own(1)

    cp_agg.wait()
    row = lax.broadcasted_iota(jnp.int32, (BS, BS), 0)
    for b in range(NB):
        which = agg_v[b:b + 1, :]
        cols = slice(b * BS, (b + 1) * BS)
        oh[:, cols] = jnp.where(row == which, 1.0, 0.0).astype(BF16)
        for side in range(NZH):
            target = jnp.where((row // 16) % 2 == core, 32 * (row // 32) + 16 * side + row % 16, -1)
            ohs[side, :, cols] = jnp.where(target == which, 1.0, 0.0).astype(BF16)

    couple(1)
    mx[2, 0] = take_peak(1)
    send_peak(2)
    split_own(2)

    for d in range(1, NQ):
        inv_copy(d).wait_recv()
    for j in range(NQ):
        for i in range(NY):
            block = inv_r[j, i]
            high = block.astype(BF16)
            cols = slice(i * BS, (i + 1) * BS)
            wc[j * ROWS:(j + 1) * ROWS, cols] = high
            wc[BS + j * ROWS:BS + (j + 1) * ROWS, cols] = (block - high.astype(F32)).astype(BF16)

    couple(2)
    upper = 1.0 + take_peak(2)[0:1, :]

    centre = 0.625 * upper
    half_span = 0.375 * upper
    spread_ratio = 5.0 / 3.0
    weight_prev = 0.6
    zero = jnp.zeros_like(upper)
    delta = [1.0 / centre, zero, zero]
    sigma = list(delta)
    rho = [zero + 1.0, zero, zero, zero]

    def apply(rho, delta):
        rho = list(rho)
        for j in range(3):
            rho[j] = rho[j] - delta[j]
            rho[j + 1] = rho[j + 1] + delta[j]
        return rho

    for _ in range(SWEEPS):
        rho = apply(rho, delta)
        weight = 1.0 / (2.0 * spread_ratio - weight_prev)
        gain = 2.0 * weight / half_span
        delta = [weight * weight_prev * delta[j] + gain * rho[j] for j in range(3)]
        sigma = [sigma[j] + delta[j] for j in range(3)]
        weight_prev = weight
    rho = apply(rho, delta)

    parts = []
    for b in range(NB):
        residual = rho[0] * loads_v[b] + rho[1] * ksum[0, b] + rho[2] * ksum[1, b] + rho[3] * ksum[2, b]
        res_v[b] = residual
        parts.append(split(residual))
    pair = dot(jnp.concatenate(parts, axis=1), oh[...], NT)
    part = pair[:VEC] + pair[VEC:]

    slot = (x - zl + NX) % NX
    a_copy = rcopy(p_s, a_r.at[slot], a_ss, a_rs.at[slot], at(y, zl, core, zl, zh))
    owner = x == zl

    def b_copy(d):
        return rcopy(b_r.at[zh], b_r.at[zh], b_ss.at[d], b_rs.at[zh], z_peer(d))

    def b_arrival(side):
        return rcopy(b_r.at[side], b_r.at[side], b_ss.at[0], b_rs.at[side], z_peer(1))

    p_s[...] = part

    @pl.when(jnp.logical_not(owner))
    def _():
        a_copy.start()

    @pl.when(owner)
    def _():
        total = p_s[...]
        for d in range(1, NX):
            rcopy(p_s, a_r.at[d], a_ss, a_rs.at[d], at(y, zl, core, zl, zh)).wait_recv()
            total = total + a_r[d]
        b_r[zh] = total
        for d in range(1, NZ):
            b_copy(d).start()

    cp_res = pltpu.make_async_copy(res_v, res_h, lsem.at[8])
    cp_res.start()

    @pl.when(owner)
    def _():
        b_arrival(1 - zh).wait_recv()

    @pl.when(jnp.logical_not(owner))
    def _():
        for side in range(NZH):
            b_arrival(side).wait_recv()

    c_r[y] = b_r[0] + b_r[1]

    def c_copy(d):
        return rcopy(c_r.at[y], c_r.at[y], c_ss.at[d], c_rs.at[d], y_peer(d))

    def c_arrival(d):
        came = (y - d + NY) % NY
        return rcopy(c_r.at[came], c_r.at[came], c_ss.at[d], c_rs.at[d], y_peer(d))

    for d in range(1, NY):
        c_copy(d).start()
    for d in range(1, NY):
        c_arrival(d).wait_recv()
    fields = jnp.concatenate([split(c_r[i]) for i in range(NY)], axis=1)
    d_r[0] = folded(dot(fields, wc[...], NT))

    def d_copy(d):
        return rcopy(d_r.at[0], d_r.at[d], d_ss.at[d], d_rs.at[d], xk_peer(d))

    for d in range(1, NQ):
        d_copy(d).start()
    for d in range(1, NQ):
        d_copy(d).wait_recv()
    total = d_r[0]
    for d in range(1, NQ):
        total = total + d_r[d]
    e_r[0] = total
    e_copy = rcopy(e_r.at[0], e_r.at[1], e_ss, e_rs, at(y, zl, core, x, 1 - zh))
    e_copy.start()

    def spread(values, side):
        pair = dot(split(values), ohs[side], NN)
        return pair[:VEC] + pair[VEC:]

    near = spread(total, zh)
    for b in range(NB):
        corr_v[b] = (sigma[0] * own[0, b] + sigma[1] * own[1, b] + sigma[2] * own[2, b]
                     + near[:, b * BS:(b + 1) * BS])
    e_copy.wait_recv()
    far = spread(e_r[1], 1 - zh)
    for b in range(NB):
        corr_v[b] = corr_v[b] + far[:, b * BS:(b + 1) * BS]
    cp_corr = pltpu.make_async_copy(corr_v, corr_h, lsem.at[9])
    cp_corr.start()

    for k in range(SWEEPS + 1):
        pl.when(w > 0)(lambda k=k: to_left(k).wait_send())
        pl.when(w < N_WIDE - 1)(lambda k=k: to_right(k).wait_send())
    for d in range(1, 8):
        for stage in range(3):
            peak_copy(stage, d).wait_send()
        inv_copy(d).wait_send()
        c_copy(d).wait_send()
        d_copy(d).wait_send()

    @pl.when(owner)
    def _():
        for d in range(1, NZ):
            b_copy(d).wait_send()

    @pl.when(jnp.logical_not(owner))
    def _():
        a_copy.wait_send()

    e_copy.wait_send()
    cp_res.wait()
    cp_corr.wait()


def shards(loads, diagonal, stiffness, neighbors, slot_mask, send_list, aggregate, coarse_inverse):
    smem = pl.BlockSpec(memory_space=pltpu.SMEM)
    hbm = pl.BlockSpec(memory_space=pl.ANY)
    field = (NB, VEC, BS)
    dma = pltpu.SemaphoreType.DMA
    return pl.pallas_call(
        kernel,
        out_shape=(jax.ShapeDtypeStruct(field, F32), jax.ShapeDtypeStruct(field, F32)),
        in_specs=[smem, smem, smem, hbm, hbm, hbm, hbm, hbm],
        out_specs=(hbm, hbm),
        scratch_shapes=[
            pltpu.VMEM(field, F32),
            pltpu.VMEM((NB, BS), F32),
            pltpu.VMEM((NB, NS, BS, BS), F32),
            pltpu.VMEM((NB, BS), jnp.int32),
            pltpu.VMEM((ROWS, NQ * NY * BS), F32),
            pltpu.VMEM((3,) + field, F32),
            pltpu.VMEM((3,) + field, F32),
            pltpu.VMEM((3,) + field, F32),
            pltpu.VMEM((3,) + field, F32),
            pltpu.VMEM((2 * NB, 2 * VEC, BS), BF16),
            pltpu.VMEM((NB, 2 * BS, NS * BS), BF16),
            pltpu.VMEM((3, 8, 8, BS), F32),
            pltpu.VMEM((NQ, NY, ROWS, BS), F32),
            pltpu.VMEM((NQ, NY, ROWS, BS), F32),
            pltpu.VMEM((2 * BS, NY * BS), BF16),
            pltpu.VMEM((BS, NB * BS), BF16),
            pltpu.VMEM((NZH, BS, NB * BS), BF16),
            pltpu.VMEM((VEC, BS), F32),
            pltpu.VMEM((NX, VEC, BS), F32),
            pltpu.VMEM((NZH, VEC, BS), F32),
            pltpu.VMEM((NY, VEC, BS), F32),
            pltpu.VMEM((NQ, VEC, BS), F32),
            pltpu.VMEM((2, VEC, BS), F32),
            pltpu.VMEM(field, F32),
            pltpu.VMEM(field, F32),
            dma((10,)),
            dma((3, 2)), dma((3, 2)),
            dma((3, 8)), dma((3, 8)),
            dma((8,)), dma((8,)),
            dma(()), dma((NX,)),
            dma((8,)), dma((NZH,)),
            dma((8,)), dma((8,)),
            dma((8,)), dma((8,)),
            dma(()), dma(()),
        ],
        compiler_params=pltpu.CompilerParams(collective_id=0, has_side_effects=True, vmem_limit_bytes=24 * 1024 * 1024),
    )(neighbors, slot_mask, send_list, loads, diagonal, stiffness, aggregate, coarse_inverse)


def solution(mesh):
    both = ("wide", "narrow")
    return jax.shard_map(
        shards,
        mesh=mesh,
        in_specs=(
            P(both, None, None),
            P(both, None),
            P(both, None, None, None),
            P(both, None),
            P(both, None),
            P(both),
            P(both, None),
            P(both, None),
        ),
        out_specs=(P(both, None, None), P(both, None, None)),
        check_vma=False,
    )
```

time: 1650 us -> 62.7 us (0.04)
  blocking collectives: 1500 us -> 0 us
  waiting for transfers between devices: 100 us -> 0 us
  Pallas kernels: 0 us -> 54 us
    all_gather x2 -> x0, blocking collectives: 1390 us -> none  [the longest x1 1350 us: shards(): lax.all_gather(owned_sums, ('wide', 'narrow'), axis=1, tiled=True)]
    pmax x1 -> x0, blocking collectives: 106 us -> none  [shards(): upper_bound = 1.0 + lax.pmax(local_peak, ('wide', 'narrow'))]
    unnamed x2 -> x0, waiting for transfers between devices: 92.9 us -> none
    pallas_call x0 -> x1, Pallas kernels: none -> 54 us  [shards(): pl.pallas_call(kernel, out_shape=(jax.ShapeDtypeStruct(field, F32), jax.S...]
  transfers between devices with their start and end apart: 7 -> 0, of which waited for: 4 -> 0; matrix products, arithmetic and copies ran while one was open for 0% -> 0% of each run, Pallas kernels for 0% -> 0%
where the time goes in v1:
time: 62.7 us; the launch traced here: 62.4 us
  Pallas kernels  54 us (86%)
  local copies, waits for them, and re-layouts  7.68 us (12%)
  between operations  0.66 us (1%)
    pallas_call x1, Pallas kernels, shards(): pl.pallas_call(kernel, out_shape=(jax.ShapeDtypeStruct(field, F32), jax.S...  54 us
    unnamed x18, local copies, waits for them, and re-layouts  7.68 us

profile of v1, /device:TPU:1, one launch (start us, length us, event | category | flops | bytes accessed | tf_op | source)
XLA Modules:
  0.0 62.4 jit_solution(11115218541402302500)
XLA Ops:
  0.6 0.0 copy-start
  0.6 1.2 %copy-done = f32[4,4,128,128]{3,2,1,0:T(8,128)S(1)} copy-done((f32[4,4,128,128]{3,2,1,0:T(8,128)S(1)}, f32[4,4,128,128]{3,2,1,0:T(8,128)}, u32[]{:S(2)}) %copy-start) | copy-done | bytes 1048600
  1.9 0.0 copy-start.1
  1.9 1.0 %copy-done.1 = f32[16,8192]{1,0:T(8,128)S(1)} copy-done((f32[16,8192]{1,0:T(8,128)S(1)}, f32[16,8192]{1,0:T(8,128)}, u32[]{:S(2)}) %copy-start.1) | copy-done | bytes 524312
  2.9 0.0 copy-start.2
  2.9 0.8 %copy-done.2 = f32[4,24,128]{2,1,0:T(8,128)S(1)} copy-done((f32[4,24,128]{2,1,0:T(8,128)S(1)}, f32[4,24,128]{2,1,0:T(8,128)}, u32[]{:S(2)}) %copy-start.2) | copy-done | bytes 49176
  3.7 0.0 copy-start.3
  3.7 0.7 %copy-done.3 = s32[4,4]{1,0:T(4,128)S(1)} copy-done((s32[4,4]{1,0:T(4,128)S(1)}, s32[4,4]{1,0:T(4,128)}, u32[]{:S(2)}) %copy-start.3) | copy-done | bytes 88
  4.4 0.0 copy-start.4
  4.4 0.7 %copy-done.4 = s32[4,4]{1,0:T(4,128)S(1)} copy-done((s32[4,4]{1,0:T(4,128)S(1)}, s32[4,4]{1,0:T(4,128)}, u32[]{:S(2)}) %copy-start.4) | copy-done | bytes 88
  5.1 0.0 copy-start.5
  5.1 0.7 %copy-done.5 = f32[4,128]{1,0:T(4,128)S(1)} copy-done((f32[4,128]{1,0:T(4,128)S(1)}, f32[4,128]{1,0:T(4,128)}, u32[]{:S(2)}) %copy-start.5) | copy-done | bytes 2072
  5.7 0.0 copy-start.6
  5.7 0.7 %copy-done.6 = s32[4,128]{1,0:T(4,128)S(1)} copy-done((s32[4,128]{1,0:T(4,128)S(1)}, s32[4,128]{1,0:T(4,128)}, u32[]{:S(2)}) %copy-start.6) | copy-done | bytes 2072
  6.4 0.0 copy-start.7
  6.4 0.7 %copy-done.7 = s32[4]{0:T(128)S(1)} copy-done((s32[4]{0:T(128)S(1)}, s32[4]{0:T(128)}, u32[]{:S(2)}) %copy-start.7) | copy-done | bytes 40
  7.1 54.0 %shard_map.95 = (f32[4,24,128]{2,1,0:T(8,128)S(1)}, f32[4,24,128]{2,1,0:T(8,128)S(1)}) custom-call(s32[4,4]{1,0:T(4,128)S(1)} %copy-done.3, s32[4,4]{1,0:T(4,128)S(1)} %copy-done.4, s32[4]{0:T(128)S(1)} %copy-done.7, f32[4,24,128]{2,1,0:T(8,128)S(1)} %copy-done.2, f32[4,128]{1,0:T(4,128)S(1)} %copy-done.5, f32[4,4,128,128]{3,2,1,0:T(8,128)S(1)} %copy-done, ...), custom_call_target="tpu_custom_call" | custom-call | tf_op jit(solution)/shard_map/pallas_call | solution.py:378
  61.1 0.6 copy.12
  61.8 0.6 copy.13
Async XLA Ops:
  0.6 1.2 %copy-start = (f32[4,4,128,128]{3,2,1,0:T(8,128)S(1)}, f32[4,4,128,128]{3,2,1,0:T(8,128)}, u32[]{:S(2)}) copy-start(f32[4,4,128,128]{3,2,1,0:T(8,128)} %stiff_h.1) | copy-start | bytes 3145732
  1.9 1.0 %copy-start.1 = (f32[16,8192]{1,0:T(8,128)S(1)}, f32[16,8192]{1,0:T(8,128)}, u32[]{:S(2)}) copy-start(f32[16,8192]{1,0:T(8,128)} %inv_h.1) | copy-start | bytes 1572868
  2.9 0.8 %copy-start.2 = (f32[4,24,128]{2,1,0:T(8,128)S(1)}, f32[4,24,128]{2,1,0:T(8,128)}, u32[]{:S(2)}) copy-start(f32[4,24,128]{2,1,0:T(8,128)} %loads_h.1) | copy-start | bytes 147460
  3.7 0.7 %copy-start.3 = (s32[4,4]{1,0:T(4,128)S(1)}, s32[4,4]{1,0:T(4,128)}, u32[]{:S(2)}) copy-start(s32[4,4]{1,0:T(4,128)} %nbr.1) | copy-start | bytes 196
  4.4 0.7 %copy-start.4 = (s32[4,4]{1,0:T(4,128)S(1)}, s32[4,4]{1,0:T(4,128)}, u32[]{:S(2)}) copy-start(s32[4,4]{1,0:T(4,128)} %msk.1) | copy-start | bytes 196
  5.1 0.7 %copy-start.5 = (f32[4,128]{1,0:T(4,128)S(1)}, f32[4,128]{1,0:T(4,128)}, u32[]{:S(2)}) copy-start(f32[4,128]{1,0:T(4,128)} %diag_h.1) | copy-start | bytes 6148
  5.7 0.7 %copy-start.6 = (s32[4,128]{1,0:T(4,128)S(1)}, s32[4,128]{1,0:T(4,128)}, u32[]{:S(2)}) copy-start(s32[4,128]{1,0:T(4,128)} %agg_h.1) | copy-start | bytes 6148
  6.4 0.7 %copy-start.7 = (s32[4]{0:T(128)S(1)}, s32[4]{0:T(128)}, u32[]{:S(2)}) copy-start(s32[4]{0:T(128)} %snd.1) | copy-start | bytes 52

commit v2 on v1

v2 whole, which is shorter than its diff:
```python
import jax
import jax.numpy as jnp
from jax import lax
from jax.experimental import pallas as pl
from jax.experimental.pallas import tpu as pltpu
from jax.sharding import PartitionSpec as P

F32 = jnp.float32
BF16 = jnp.bfloat16
MESH = pl.DeviceIdType.MESH
NB, NS, VEC, BS = 4, 4, 24, 128
NX, NY, NZL, NZH = 4, 8, 4, 2
NZ = NZL * NZH
NG = 2 * NX
N_WIDE = NY * NZL * 2
SWEEPS = 2
ROWS = 16
NT = (((1,), (1,)), ((), ()))
NN = (((1,), (0,)), ((), ()))


def split(value):
    high = value.astype(BF16).astype(F32)
    return jnp.concatenate([high, value - high], axis=0).astype(BF16)


def dot(a, b, dims):
    return lax.dot_general(a, b, dims, preferred_element_type=F32)


def folded(full):
    half = full.shape[0] // 2
    cols = full.shape[1] // 2
    return full[:half, :cols] + (full[:half, cols:] + full[half:, :cols])


def roll(value, lanes):
    return value if lanes % BS == 0 else pltpu.roll(value, lanes % BS, 1)


def regroup(tiles, count, width):
    lane = lax.broadcasted_iota(jnp.int32, tiles[0].shape, 1) // width
    out = []
    for i in range(count):
        acc = None
        for j, tile in enumerate(tiles):
            moved = roll(tile, width * (j - i))
            acc = moved if acc is None else jnp.where(lane == j, moved, acc)
        out.append(acc)
    return out


def hops(step, size):
    return min(step, size - step)


def kernel(nbr_h, msk_h, snd_h, loads_h, diag_h, stiff_h, agg_h, inv_h, corr_v, res_v,
           nbr, msk, snd, loads_v, diag_v, stiff_v, agg_v, inv_v, own, ksum, sbuf, ghost, exts, w2,
           mx, inv_s, inv_r, wc, oh, ohs, i_s, i_r, c_r, d_s, d_r,
           lsem, halo_ss, halo_rs, mx_ss, mx_rs, inv_ss, inv_rs, i_ss, i_rs, c_ss, c_rs, d_ss, d_rs):
    w = lax.axis_index("wide")
    n = lax.axis_index("narrow")
    core = w % 2
    zl = (w // 2) % NZL
    y = w // (2 * NZL)
    x = n // NZH
    zh = n % NZH
    z = zh * NZL + zl
    g = NX * core + x

    cp_loads = pltpu.make_async_copy(loads_h, loads_v, lsem.at[0])
    cp_diag = pltpu.make_async_copy(diag_h, diag_v, lsem.at[1])
    cp_stiff = [pltpu.make_async_copy(stiff_h.at[b], stiff_v.at[b], lsem.at[2 + b]) for b in range(NB)]
    cp_inv = pltpu.make_async_copy(inv_h, inv_v, lsem.at[6])
    cp_agg = pltpu.make_async_copy(agg_h, agg_v, lsem.at[7])
    cp_snd = pltpu.make_async_copy(snd_h, snd, lsem.at[8])
    cp_msk = pltpu.make_async_copy(msk_h, msk, lsem.at[9])
    cp_nbr = pltpu.make_async_copy(nbr_h, nbr, lsem.at[10])
    for cp in [cp_loads, cp_diag, cp_snd, cp_msk, cp_nbr] + cp_stiff + [cp_inv, cp_agg]:
        cp.start()

    def at(y_, zl_, core_, x_, zh_):
        return ((y_ * NZL + zl_) * 2 + core_, x_ * NZH + zh_)

    def g_peer(d):
        other = (g + d) % NG
        return at(y, zl, other // NX, other % NX, zh)

    def z_peer(d):
        other = (z + d) % NZ
        return at(y, other % NZL, core, x, other // NZL)

    def y_peer(d):
        return at((y + d) % NY, zl, core, x, zh)

    pending = []

    def rcopy(src, dst, ss, rs, dev):
        return pltpu.make_async_remote_copy(src_ref=src, dst_ref=dst, send_sem=ss, recv_sem=rs,
                                            device_id=dev, device_id_type=MESH)

    barrier = pltpu.get_barrier_semaphore()

    def greet(dev):
        pl.semaphore_signal(barrier, inc=1, device_id=dev, device_id_type=MESH)

    left_far = jnp.logical_and(core == 0, w > 0)
    right_far = jnp.logical_and(core == 1, w < N_WIDE - 1)
    pl.when(left_far)(lambda: greet((w - 1, n)))
    pl.when(right_far)(lambda: greet((w + 1, n)))
    for d in range(1, 8):
        greet(g_peer(d))
        greet(z_peer(d))
        greet(y_peer(d))

    @pl.when(w == 0)
    def _():
        ghost[:, 0:2] = jnp.zeros((3, 2, VEC, BS), F32)

    @pl.when(w == N_WIDE - 1)
    def _():
        ghost[:, 2:4] = jnp.zeros((3, 2, VEC, BS), F32)

    cp_loads.wait()
    cp_diag.wait()
    rdiag = [1.0 / diag_v[b:b + 1, :] for b in range(NB)]
    for b in range(NB):
        own[0, b] = loads_v[b] * rdiag[b]
    cp_snd.wait()

    def to_left(k):
        return rcopy(sbuf.at[k, pl.ds(0, 2)], ghost.at[k, pl.ds(2, 2)], halo_ss.at[k, 0], halo_rs.at[k, 0], (w - 1, n))

    def to_right(k):
        return rcopy(sbuf.at[k, pl.ds(2, 2)], ghost.at[k, pl.ds(0, 2)], halo_ss.at[k, 1], halo_rs.at[k, 1], (w + 1, n))

    def fill_halo(k):
        for j in range(4):
            sbuf[k, j] = own[k, snd[j]]

    def send_halo(k):
        pl.when(w > 0)(lambda: to_left(k).start())
        pl.when(w < N_WIDE - 1)(lambda: to_right(k).start())
        pending.append(lambda: pl.when(w > 0)(lambda: to_left(k).wait_send()))
        pending.append(lambda: pl.when(w < N_WIDE - 1)(lambda: to_right(k).wait_send()))

    def wait_halo(k):
        pl.when(w < N_WIDE - 1)(lambda: to_left(k).wait_recv())
        pl.when(w > 0)(lambda: to_right(k).wait_recv())

    fill_halo(0)

    @pl.when(jnp.logical_or(left_far, right_far))
    def _():
        pl.semaphore_wait(barrier, 22)

    @pl.when(jnp.logical_not(jnp.logical_or(left_far, right_far)))
    def _():
        pl.semaphore_wait(barrier, 21)

    send_halo(0)

    cp_msk.wait()
    ones = jnp.ones((16, BS), BF16)
    peak = None
    for b in range(NB):
        cp_stiff[b].wait()
        total = None
        for s in range(NS):
            block = stiff_v[b, s] * msk[b, s].astype(F32)
            size = jnp.abs(block)
            total = size if total is None else total + size
            block = block.T
            high = block.astype(BF16)
            w2[b, s * BS:(s + 1) * BS, 0:BS] = high
            w2[b, s * BS:(s + 1) * BS, BS:2 * BS] = (block - high.astype(F32)).astype(BF16)
        sums = dot(ones, split(total), NT)[:8]
        ratio = (sums[:, :BS] + sums[:, BS:]) / diag_v[b:b + 1, :]
        peak = ratio if peak is None else jnp.maximum(peak, ratio)
    mx[0, 0] = jnp.broadcast_to(jnp.max(peak, axis=1, keepdims=True), (8, BS))

    def peak_copy(stage, d):
        dev = (g_peer, z_peer, y_peer)[stage](d)
        row = pl.ds(0, 1)
        return rcopy(mx.at[stage, 0, row], mx.at[stage, d, row], mx_ss.at[stage, d], mx_rs.at[stage, d], dev)

    def send_peak(stage):
        for d in (4, 3, 5, 2, 6, 1, 7):
            peak_copy(stage, d).start()
            pending.append(peak_copy(stage, d).wait_send)

    def take_peak(stage):
        for d in range(1, 8):
            peak_copy(stage, d).wait_recv()
        top = mx[stage, 0, 0:1]
        for d in range(1, 8):
            top = jnp.maximum(top, mx[stage, d, 0:1])
        return top

    send_peak(0)

    def split_own(k):
        for b in range(NB):
            exts[b] = split(own[k, b])

    split_own(0)

    cp_inv.wait()
    for i in range(NY):
        for c in range(2):
            cols = [(NG * i + 2 * j + c) * BS for j in range(NZL)]
            for j, piece in enumerate(regroup([inv_v[:, col:col + BS] for col in cols], NX, 32)):
                inv_s[NX * c + j, i] = piece

    def inv_copy(d):
        other = (g + d) % NG
        return rcopy(inv_s.at[other], inv_r.at[g], inv_ss.at[d], inv_rs.at[d], g_peer(d))

    def send_inv(steps):
        for d in steps:
            inv_copy(d).start()
            pending.append(inv_copy(d).wait_send)

    send_inv((4, 1, 7))
    inv_r[g] = inv_s[g]
    cp_nbr.wait()

    def couple(k):
        wait_halo(k)
        for j in range(4):
            exts[NB + j] = split(ghost[k, j])
        for b in range(NB):
            fields = jnp.concatenate([exts[nbr[b, s]] for s in range(NS)], axis=1)
            coupled = folded(dot(fields, w2[b], NN))
            ksum[k, b] = coupled
            if k < SWEEPS:
                own[k + 1, b] = coupled * rdiag[b]
        if k < SWEEPS:
            fill_halo(k + 1)
            send_halo(k + 1)

    couple(0)
    mx[1, 0, 0:1] = take_peak(0)
    send_peak(1)
    send_inv((2, 6))
    split_own(1)

    cp_agg.wait()
    row = lax.broadcasted_iota(jnp.int32, (BS, BS), 0)
    turned = 32 * ((row // ROWS) % NX) + ROWS * (row // 64) + row % ROWS
    for b in range(NB):
        which = agg_v[b:b + 1, :]
        cols = slice(b * BS, (b + 1) * BS)
        oh[:, cols] = jnp.where(row == which, 1.0, 0.0).astype(BF16)
        ohs[:, cols] = jnp.where(turned == which, 1.0, 0.0).astype(BF16)

    couple(1)
    mx[2, 0, 0:1] = take_peak(1)
    send_peak(2)
    send_inv((3, 5))
    split_own(2)
    couple(2)
    upper = 1.0 + take_peak(2)

    centre = 0.625 * upper
    half_span = 0.375 * upper
    spread_ratio = 5.0 / 3.0
    weight_prev = 0.6
    zero = jnp.zeros_like(upper)
    delta = [1.0 / centre, zero, zero]
    sigma = list(delta)
    rho = [zero + 1.0, zero, zero, zero]

    def apply(rho, delta):
        rho = list(rho)
        for j in range(3):
            rho[j] = rho[j] - delta[j]
            rho[j + 1] = rho[j + 1] + delta[j]
        return rho

    for _ in range(SWEEPS):
        rho = apply(rho, delta)
        weight = 1.0 / (2.0 * spread_ratio - weight_prev)
        gain = 2.0 * weight / half_span
        delta = [weight * weight_prev * delta[j] + gain * rho[j] for j in range(3)]
        sigma = [sigma[j] + delta[j] for j in range(3)]
        weight_prev = weight
    rho = apply(rho, delta)

    parts = []
    for b in range(NB):
        residual = rho[0] * loads_v[b] + rho[1] * ksum[0, b] + rho[2] * ksum[1, b] + rho[3] * ksum[2, b]
        res_v[b] = residual
        parts.append(split(residual))
    pair = dot(jnp.concatenate(parts, axis=1), oh[...], NT)
    part = pair[:VEC] + pair[VEC:]

    for j, piece in enumerate(regroup([part[8 * i:8 * i + 8] for i in range(3)], NX, 32)):
        i_s[j] = piece
    side = NX * zh + x
    i_r[zl, side] = i_s[x]
    plane = [(dx, dz) for dx in range(NX) for dz in range(NZ) if dx or dz]
    plane.sort(key=lambda p: -hops(p[0], NX) - hops(p[1], NZ))

    def i_copy(dx, dz):
        other = (z + dz) % NZ
        ox = (x + dx) % NX
        k = NZ * dx + dz
        return rcopy(i_s.at[ox], i_r.at[zl, side], i_ss.at[k], i_rs.at[k],
                     at(y, other % NZL, core, ox, other // NZL))

    def i_arrival(dx, dz):
        came = (z + NZ - dz) % NZ
        cx = (x + NX - dx) % NX
        k = NZ * dx + dz
        slot = i_r.at[came % NZL, NX * (came // NZL) + cx]
        return rcopy(slot, slot, i_ss.at[k], i_rs.at[k], z_peer(1))

    for dx, dz in plane:
        i_copy(dx, dz).start()
        pending.append(i_copy(dx, dz).wait_send)

    for b in range(NB):
        corr_v[b] = sigma[0] * own[0, b] + sigma[1] * own[1, b] + sigma[2] * own[2, b]
    for d in range(1, NG):
        inv_copy(d).wait_recv()
    for j in range(NG):
        for i in range(NY):
            block = inv_r[j, i]
            high = block.astype(BF16)
            cols = slice(i * BS, (i + 1) * BS)
            wc[j * ROWS:(j + 1) * ROWS, cols] = high
            wc[BS + j * ROWS:BS + (j + 1) * ROWS, cols] = (block - high.astype(F32)).astype(BF16)

    for dx, dz in reversed(plane):
        i_arrival(dx, dz).wait_recv()
    tiles = []
    for j in range(NZL):
        total = i_r[j, 0]
        for k in range(1, 2 * NX):
            total = total + i_r[j, k]
        tiles.append(total)
    c_r[y] = jnp.concatenate(regroup(tiles, 3, 32), axis=0)

    def c_copy(d):
        return rcopy(c_r.at[y], c_r.at[y], c_ss.at[d], c_rs.at[d], y_peer(d))

    def c_arrival(d):
        came = (y - d + NY) % NY
        return rcopy(c_r.at[came], c_r.at[came], c_ss.at[d], c_rs.at[d], y_peer(d))

    for d in (4, 3, 5, 2, 6, 1, 7):
        c_copy(d).start()
        pending.append(c_copy(d).wait_send)
    for d in (1, 7, 2, 6, 3, 5, 4):
        c_arrival(d).wait_recv()
    fields = jnp.concatenate([split(c_r[i]) for i in range(NY)], axis=1)
    coarse = folded(dot(fields, wc[...], NT))

    low = lax.broadcasted_iota(jnp.int32, (8, BS), 1) < 64
    t0, t1, t2 = coarse[0:8], coarse[8:16], coarse[16:24]
    u0, u1, u2 = roll(t0, 64), roll(t1, 64), roll(t2, 64)
    d_s[0] = jnp.concatenate([jnp.where(low, t0, u1), jnp.where(low[:4], t2[0:4], u2[4:8])], axis=0)
    d_s[1] = jnp.concatenate([jnp.where(low, u0, t1), jnp.where(low[:4], u2[0:4], t2[4:8])], axis=0)
    d_r[zh, g] = d_s[core]
    around = [(dg, dh) for dg in range(NG) for dh in range(NZH) if dg or dh]
    around.sort(key=lambda p: -4 * p[1] - hops(p[0], NG))

    def d_copy(dg, dh):
        other = (g + dg) % NG
        k = NG * dh + dg
        return rcopy(d_s.at[other // NX], d_r.at[zh, g], d_ss.at[k], d_rs.at[k],
                     at(y, zl, other // NX, other % NX, (zh + dh) % NZH))

    def d_arrival(dg, dh):
        slot = d_r.at[(zh + dh) % NZH, (g + NG - dg) % NG]
        k = NG * dh + dg
        return rcopy(slot, slot, d_ss.at[k], d_rs.at[k], z_peer(1))

    for dg, dh in around:
        d_copy(dg, dh).start()
        pending.append(d_copy(dg, dh).wait_send)
    for wait in pending:
        wait()
    for dg, dh in reversed(around):
        d_arrival(dg, dh).wait_recv()
    sums = []
    for h in range(NZH):
        total = d_r[h, 0]
        for j in range(1, NG):
            total = total + d_r[h, j]
        sums.append(total)

    def tail(value):
        return jnp.concatenate([value[8:12], roll(value[8:12], 64)], axis=0)

    p0, p1 = sums[0][:8], sums[1][:8]
    q0, q1 = tail(sums[0]), tail(sums[1])
    solved = jnp.concatenate([jnp.where(low, p0, roll(p1, 64)), jnp.where(low, roll(p0, 64), p1),
                              jnp.where(low, q0, roll(q1, 64))], axis=0)
    pair = dot(split(solved), ohs[...], NN)
    for b in range(NB):
        cols = slice(b * BS, (b + 1) * BS)
        corr_v[b] = corr_v[b] + (pair[:VEC, cols] + pair[VEC:, cols])


def shards(loads, diagonal, stiffness, neighbors, slot_mask, send_list, aggregate, coarse_inverse):
    hbm = pl.BlockSpec(memory_space=pltpu.HBM)
    vmem = pl.BlockSpec(memory_space=pltpu.VMEM)
    field = (NB, VEC, BS)
    dma = pltpu.SemaphoreType.DMA
    corr, res = pl.pallas_call(
        kernel,
        out_shape=(pltpu.VMEM(field, F32), pltpu.VMEM(field, F32)),
        in_specs=[hbm] * 8,
        out_specs=(vmem, vmem),
        scratch_shapes=[
            pltpu.SMEM((NB, NS), jnp.int32),
            pltpu.SMEM((NB, NS), jnp.int32),
            pltpu.SMEM((4,), jnp.int32),
            pltpu.VMEM(field, F32),
            pltpu.VMEM((NB, BS), F32),
            pltpu.VMEM((NB, NS, BS, BS), F32),
            pltpu.VMEM((NB, BS), jnp.int32),
            pltpu.VMEM((ROWS, NG * NY * BS), F32),
            pltpu.VMEM((3,) + field, F32),
            pltpu.VMEM((3,) + field, F32),
            pltpu.VMEM((3,) + field, F32),
            pltpu.VMEM((3,) + field, F32),
            pltpu.VMEM((2 * NB, 2 * VEC, BS), BF16),
            pltpu.VMEM((NB, NS * BS, 2 * BS), BF16),
            pltpu.VMEM((3, 8, 8, BS), F32),
            pltpu.VMEM((NG, NY, ROWS, BS), F32),
            pltpu.VMEM((NG, NY, ROWS, BS), F32),
            pltpu.VMEM((2 * BS, NY * BS), BF16),
            pltpu.VMEM((BS, NB * BS), BF16),
            pltpu.VMEM((BS, NB * BS), BF16),
            pltpu.VMEM((NX, 8, BS), F32),
            pltpu.VMEM((NZL, 2 * NX, 8, BS), F32),
            pltpu.VMEM((NY, VEC, BS), F32),
            pltpu.VMEM((2, 12, BS), F32),
            pltpu.VMEM((NZH, NG, 12, BS), F32),
            dma((11,)),
            dma((3, 2)), dma((3, 2)),
            dma((3, 8)), dma((3, 8)),
            dma((8,)), dma((8,)),
            dma((32,)), dma((32,)),
            dma((8,)), dma((8,)),
            dma((16,)), dma((16,)),
        ],
        compiler_params=pltpu.CompilerParams(collective_id=0, has_side_effects=True, vmem_limit_bytes=58 * 1024 * 1024),
    )(neighbors, slot_mask, send_list, loads, diagonal, stiffness, aggregate, coarse_inverse)
    return corr, res


def solution(mesh):
    both = ("wide", "narrow")
    return jax.shard_map(
        shards,
        mesh=mesh,
        in_specs=(
            P(both, None, None),
            P(both, None),
            P(both, None, None, None),
            P(both, None),
            P(both, None),
            P(both),
            P(both, None),
            P(both, None),
        ),
        out_specs=(P(both, None, None), P(both, None, None)),
        check_vma=False,
    )
```

time: 62.7 us -> 50.6 us (0.81)
  local copies, waits for them, and re-layouts: 7.68 us -> 1.24 us
  Pallas kernels: 54 us -> 48.6 us
    unnamed x18 -> x2, local copies, waits for them, and re-layouts: 7.68 us -> 1.24 us
    pallas_call x1, Pallas kernels: 54 us -> 48.6 us  [shards(): pl.pallas_call(kernel, out_shape=(pltpu.VMEM(field, F32), pltpu.VMEM(fiel...]
where the time goes in v2:
time: 50.6 us; the launch traced here: 50.5 us
  Pallas kernels  48.6 us (96%)
  local copies, waits for them, and re-layouts  1.24 us (2%)
  between operations  0.64 us (1%)
    pallas_call x1, Pallas kernels, shards(): pl.pallas_call(kernel, out_shape=(pltpu.VMEM(field, F32), pltpu.VMEM(fiel...  48.6 us
    unnamed x2, local copies, waits for them, and re-layouts  1.24 us

profile of v2, /device:TPU:1, one launch (start us, length us, event | category | flops | bytes accessed | tf_op | source)
XLA Modules:
  0.0 50.5 jit_solution(13034767140513178213)
XLA Ops:
  0.6 48.6 %shard_map.95 = (f32[4,24,128]{2,1,0:T(8,128)S(1)}, f32[4,24,128]{2,1,0:T(8,128)S(1)}) custom-call(s32[4,4]{1,0:T(4,128)} %nbr_h.1, s32[4,4]{1,0:T(4,128)} %msk_h.1, s32[4]{0:T(128)} %snd_h.1, f32[4,24,128]{2,1,0:T(8,128)} %loads_h.1, f32[4,128]{1,0:T(4,128)} %diag_h.1, f32[4,4,128,128]{3,2,1,0:T(8,128)} %stiff_h.1, s32[4,128]{1,0:T(4,128)} %agg_h.1, ...), custom_call_target="tpu_custom_call" | custom-call | tf_op jit(solution)/shard_map/pallas_call | solution.py:412
  49.3 0.6 %copy.12 = f32[4,24,128]{2,1,0:T(8,128)} copy(f32[4,24,128]{2,1,0:T(8,128)S(1)} %get-tuple-element.2) | data formatting | bytes 98304
  49.9 0.6 %copy.13 = f32[4,24,128]{2,1,0:T(8,128)} copy(f32[4,24,128]{2,1,0:T(8,128)S(1)} %get-tuple-element.3) | data formatting | bytes 98304

commit v3 on v2

--- a/solution.py
+++ b/solution.py
@@ -50,6 +50,14 @@
     return out
 
 
+def mod(value, size):
+    return lax.rem(value, jnp.int32(size))
+
+
+def div(value, size):
+    return lax.div(value, jnp.int32(size))
+
+
 def hops(step, size):
     return min(step, size - step)
 
@@ -60,11 +68,11 @@
            lsem, halo_ss, halo_rs, mx_ss, mx_rs, inv_ss, inv_rs, i_ss, i_rs, c_ss, c_rs, d_ss, d_rs):
     w = lax.axis_index("wide")
     n = lax.axis_index("narrow")
-    core = w % 2
-    zl = (w // 2) % NZL
-    y = w // (2 * NZL)
-    x = n // NZH
-    zh = n % NZH
+    core = mod(w, 2)
+    zl = mod(div(w, 2), NZL)
+    y = div(w, 2 * NZL)
+    x = div(n, NZH)
+    zh = mod(n, NZH)
     z = zh * NZL + zl
     g = NX * core + x
 
@@ -83,15 +91,15 @@
         return ((y_ * NZL + zl_) * 2 + core_, x_ * NZH + zh_)
 
     def g_peer(d):
-        other = (g + d) % NG
-        return at(y, zl, other // NX, other % NX, zh)
+        other = mod(g + d, NG)
+        return at(y, zl, div(other, NX), mod(other, NX), zh)
 
     def z_peer(d):
-        other = (z + d) % NZ
-        return at(y, other % NZL, core, x, other // NZL)
+        other = mod(z + d, NZ)
+        return at(y, mod(other, NZL), core, x, div(other, NZL))
 
     def y_peer(d):
-        return at((y + d) % NY, zl, core, x, zh)
+        return at(mod(y + d, NY), zl, core, x, zh)
 
     pending = []
 
@@ -213,7 +221,7 @@
                 inv_s[NX * c + j, i] = piece
 
     def inv_copy(d):
-        other = (g + d) % NG
+        other = mod(g + d, NG)
         return rcopy(inv_s.at[other], inv_r.at[g], inv_ss.at[d], inv_rs.at[d], g_peer(d))
 
     def send_inv(steps):
@@ -254,9 +262,16 @@
         oh[:, cols] = jnp.where(row == which, 1.0, 0.0).astype(BF16)
         ohs[:, cols] = jnp.where(turned == which, 1.0, 0.0).astype(BF16)
 
+    def pass_peak(stage):
+        mx[stage, 0, 0:1] = take_peak(stage - 1)
+        for d in (4, 3, 5, 2, 6, 1, 7):
+            peak_copy(stage, d).start()
+
+    turn = jnp.logical_or(jnp.logical_and(core == 0, zl == 0), jnp.logical_and(core == 1, zl == NZL - 1))
+    pl.when(turn)(lambda: pass_peak(2))
     couple(1)
-    mx[2, 0, 0:1] = take_peak(1)
-    send_peak(2)
+    pl.when(jnp.logical_not(turn))(lambda: pass_peak(2))
+    pending.extend(peak_copy(2, d).wait_send for d in range(1, 8))
     send_inv((3, 5))
     split_own(2)
     couple(2)
@@ -303,17 +318,17 @@
     plane.sort(key=lambda p: -hops(p[0], NX) - hops(p[1], NZ))
 
     def i_copy(dx, dz):
-        other = (z + dz) % NZ
-        ox = (x + dx) % NX
+        other = mod(z + dz, NZ)
+        ox = mod(x + dx, NX)
         k = NZ * dx + dz
         return rcopy(i_s.at[ox], i_r.at[zl, side], i_ss.at[k], i_rs.at[k],
-                     at(y, other % NZL, core, ox, other // NZL))
+                     at(y, mod(other, NZL), core, ox, div(other, NZL)))
 
     def i_arrival(dx, dz):
-        came = (z + NZ - dz) % NZ
-        cx = (x + NX - dx) % NX
+        came = mod(z + NZ - dz, NZ)
+        cx = mod(x + NX - dx, NX)
         k = NZ * dx + dz
-        slot = i_r.at[came % NZL, NX * (came // NZL) + cx]
+        slot = i_r.at[mod(came, NZL), NX * div(came, NZL) + cx]
         return rcopy(slot, slot, i_ss.at[k], i_rs.at[k], z_peer(1))
 
     for dx, dz in plane:
@@ -324,13 +339,12 @@
         corr_v[b] = sigma[0] * own[0, b] + sigma[1] * own[1, b] + sigma[2] * own[2, b]
     for d in range(1, NG):
         inv_copy(d).wait_recv()
-    for j in range(NG):
-        for i in range(NY):
-            block = inv_r[j, i]
-            high = block.astype(BF16)
-            cols = slice(i * BS, (i + 1) * BS)
-            wc[j * ROWS:(j + 1) * ROWS, cols] = high
-            wc[BS + j * ROWS:BS + (j + 1) * ROWS, cols] = (block - high.astype(F32)).astype(BF16)
+    for i in range(NY):
+        block = jnp.concatenate([inv_r[j, i] for j in range(NG)], axis=0).T
+        high = block.astype(BF16)
+        rows = slice(i * BS, (i + 1) * BS)
+        wc[rows, 0:BS] = high
+        wc[rows, BS:2 * BS] = (block - high.astype(F32)).astype(BF16)
 
     for dx, dz in reversed(plane):
         i_arrival(dx, dz).wait_recv()
@@ -346,7 +360,7 @@
         return rcopy(c_r.at[y], c_r.at[y], c_ss.at[d], c_rs.at[d], y_peer(d))
 
     def c_arrival(d):
-        came = (y - d + NY) % NY
+        came = mod(y - d + NY, NY)
         return rcopy(c_r.at[came], c_r.at[came], c_ss.at[d], c_rs.at[d], y_peer(d))
 
     for d in (4, 3, 5, 2, 6, 1, 7):
@@ -355,7 +369,7 @@
     for d in (1, 7, 2, 6, 3, 5, 4):
         c_arrival(d).wait_recv()
     fields = jnp.concatenate([split(c_r[i]) for i in range(NY)], axis=1)
-    coarse = folded(dot(fields, wc[...], NT))
+    coarse = folded(dot(fields, wc[...], NN))
 
     low = lax.broadcasted_iota(jnp.int32, (8, BS), 1) < 64
     t0, t1, t2 = coarse[0:8], coarse[8:16], coarse[16:24]
@@ -367,13 +381,13 @@
     around.sort(key=lambda p: -4 * p[1] - hops(p[0], NG))
 
     def d_copy(dg, dh):
-        other = (g + dg) % NG
+        other = mod(g + dg, NG)
         k = NG * dh + dg
-        return rcopy(d_s.at[other // NX], d_r.at[zh, g], d_ss.at[k], d_rs.at[k],
-                     at(y, zl, other // NX, other % NX, (zh + dh) % NZH))
+        return rcopy(d_s.at[div(other, NX)], d_r.at[zh, g], d_ss.at[k], d_rs.at[k],
+                     at(y, zl, div(other, NX), mod(other, NX), mod(zh + dh, NZH)))
 
     def d_arrival(dg, dh):
-        slot = d_r.at[(zh + dh) % NZH, (g + NG - dg) % NG]
+        slot = d_r.at[mod(zh + dh, NZH), mod(g + NG - dg, NG)]
         k = NG * dh + dg
         return rcopy(slot, slot, d_ss.at[k], d_rs.at[k], z_peer(1))
 
@@ -402,6 +416,15 @@
     for b in range(NB):
         cols = slice(b * BS, (b + 1) * BS)
         corr_v[b] = corr_v[b] + (pair[:VEC, cols] + pair[VEC:, cols])
+
+
+def store(corr_v, res_v, corr_h, res_h, sem):
+    one = pltpu.make_async_copy(corr_v, corr_h, sem.at[0])
+    two = pltpu.make_async_copy(res_v, res_h, sem.at[1])
+    one.start()
+    two.start()
+    one.wait()
+    two.wait()
 
 
 def shards(loads, diagonal, stiffness, neighbors, slot_mask, send_list, aggregate, coarse_inverse):
@@ -432,7 +455,7 @@
             pltpu.VMEM((3, 8, 8, BS), F32),
             pltpu.VMEM((NG, NY, ROWS, BS), F32),
             pltpu.VMEM((NG, NY, ROWS, BS), F32),
-            pltpu.VMEM((2 * BS, NY * BS), BF16),
+            pltpu.VMEM((NY * BS, 2 * BS), BF16),
             pltpu.VMEM((BS, NB * BS), BF16),
             pltpu.VMEM((BS, NB * BS), BF16),
             pltpu.VMEM((NX, 8, BS), F32),
@@ -450,7 +473,15 @@
         ],
         compiler_params=pltpu.CompilerParams(collective_id=0, has_side_effects=True, vmem_limit_bytes=58 * 1024 * 1024),
     )(neighbors, slot_mask, send_list, loads, diagonal, stiffness, aggregate, coarse_inverse)
-    return corr, res
+    corr = pltpu.with_memory_space_constraint(corr, pltpu.VMEM)
+    res = pltpu.with_memory_space_constraint(res, pltpu.VMEM)
+    return pl.pallas_call(
+        store,
+        out_shape=(jax.ShapeDtypeStruct(field, F32), jax.ShapeDtypeStruct(field, F32)),
+        in_specs=[vmem, vmem],
+        out_specs=(hbm, hbm),
+        scratch_shapes=[dma((2,))],
+    )(corr, res)
 
 
 def solution(mesh):

time: 50.6 us -> 50 us (0.988)
  local copies, waits for them, and re-layouts: 1.24 us -> 0 us
  Pallas kernels: 48.6 us -> 49.2 us
    unnamed x2 -> x0, local copies, waits for them, and re-layouts: 1.24 us -> none
    pallas_call x0 -> x1, Pallas kernels: none -> 0.66 us  [shards(): pl.pallas_call(store, out_shape=(jax.ShapeDtypeStruct(field, F32), jax.Sh...]
where the time goes in v3:
time: 50 us; the launch traced here: 49.8 us
  Pallas kernels  49.2 us (98%)
  between operations  0.64 us (1%)
    pallas_call x1, Pallas kernels, shards(): pl.pallas_call(kernel, out_shape=(pltpu.VMEM(field, F32), pltpu.VMEM(fiel...  48.5 us

profile of v3, /device:TPU:1, one launch (start us, length us, event | category | flops | bytes accessed | tf_op | source)
XLA Modules:
  0.0 49.8 jit_solution(11619221573667680726)
XLA Ops:
  0.6 48.5 %shard_map.95 = (f32[4,24,128]{2,1,0:T(8,128)S(1)}, f32[4,24,128]{2,1,0:T(8,128)S(1)}) custom-call(s32[4,4]{1,0:T(4,128)} %nbr_h.1, s32[4,4]{1,0:T(4,128)} %msk_h.1, s32[4]{0:T(128)} %snd_h.1, f32[4,24,128]{2,1,0:T(8,128)} %loads_h.1, f32[4,128]{1,0:T(4,128)} %diag_h.1, f32[4,4,128,128]{3,2,1,0:T(8,128)} %stiff_h.1, s32[4,128]{1,0:T(4,128)} %agg_h.1, ...), custom_call_target="tpu_custom_call" | custom-call | tf_op jit(solution)/shard_map/pallas_call | solution.py:435
  49.2 0.7 %shard_map.96 = (f32[4,24,128]{2,1,0:T(8,128)}, f32[4,24,128]{2,1,0:T(8,128)}) custom-call(f32[4,24,128]{2,1,0:T(8,128)S(1)} %get-tuple-element.4.corr_v, f32[4,24,128]{2,1,0:T(8,128)S(1)} %get-tuple-element.5.res_v), custom_call_target="tpu_custom_call" | custom-call | tf_op jit(solution)/shard_map/pallas_call | solution.py:478

commit v4 on v3

--- a/solution.py
+++ b/solution.py
@@ -170,18 +170,14 @@
 
     cp_msk.wait()
     ones = jnp.ones((16, BS), BF16)
+    mask = [[msk[b, s].astype(F32) for s in range(NS)] for b in range(NB)]
     peak = None
     for b in range(NB):
         cp_stiff[b].wait()
         total = None
         for s in range(NS):
-            block = stiff_v[b, s] * msk[b, s].astype(F32)
-            size = jnp.abs(block)
+            size = jnp.abs(stiff_v[b, s] * mask[b][s])
             total = size if total is None else total + size
-            block = block.T
-            high = block.astype(BF16)
-            w2[b, s * BS:(s + 1) * BS, 0:BS] = high
-            w2[b, s * BS:(s + 1) * BS, BS:2 * BS] = (block - high.astype(F32)).astype(BF16)
         sums = dot(ones, split(total), NT)[:8]
         ratio = (sums[:, :BS] + sums[:, BS:]) / diag_v[b:b + 1, :]
         peak = ratio if peak is None else jnp.maximum(peak, ratio)
@@ -206,6 +202,12 @@
         return top
 
     send_peak(0)
+    for b in range(NB):
+        for s in range(NS):
+            block = (stiff_v[b, s] * mask[b][s]).T
+            high = block.astype(BF16)
+            w2[b, s * BS:(s + 1) * BS, 0:BS] = high
+            w2[b, s * BS:(s + 1) * BS, BS:2 * BS] = (block - high.astype(F32)).astype(BF16)
 
     def split_own(k):
         for b in range(NB):
@@ -247,20 +249,27 @@
             fill_halo(k + 1)
             send_halo(k + 1)
 
+    cp_agg.wait()
+    row = lax.broadcasted_iota(jnp.int32, (BS, BS), 0)
+    turned = 32 * ((row // ROWS) % NX) + ROWS * (row // 64) + row % ROWS
+    for b in range(NB):
+        which = agg_v[b:b + 1, :]
+        cols = slice(b * BS, (b + 1) * BS)
+        oh[:, cols] = jnp.where(row == which, 1.0, 0.0).astype(BF16)
+        ohs[:, cols] = jnp.where(turned == which, 1.0, 0.0).astype(BF16)
+
+    def dealt(vector):
+        pair = dot(jnp.concatenate([split(vector[b]) for b in range(NB)], axis=1), oh[...], NT)
+        part = pair[:VEC] + pair[VEC:]
+        return regroup([part[8 * i:8 * i + 8] for i in range(3)], NX, 32)
+
+    shares = [dealt(loads_v)]
     couple(0)
     mx[1, 0, 0:1] = take_peak(0)
     send_peak(1)
     send_inv((2, 6))
     split_own(1)
-
-    cp_agg.wait()
-    row = lax.broadcasted_iota(jnp.int32, (BS, BS), 0)
-    turned = 32 * ((row // ROWS) % NX) + ROWS * (row // 64) + row % ROWS
-    for b in range(NB):
-        which = agg_v[b:b + 1, :]
-        cols = slice(b * BS, (b + 1) * BS)
-        oh[:, cols] = jnp.where(row == which, 1.0, 0.0).astype(BF16)
-        ohs[:, cols] = jnp.where(turned == which, 1.0, 0.0).astype(BF16)
+    shares.append(dealt(ksum.at[0]))
 
     def pass_peak(stage):
         mx[stage, 0, 0:1] = take_peak(stage - 1)
@@ -274,44 +283,21 @@
     pending.extend(peak_copy(2, d).wait_send for d in range(1, 8))
     send_inv((3, 5))
     split_own(2)
+    shares.append(dealt(ksum.at[1]))
     couple(2)
+    shares.append(dealt(ksum.at[2]))
     upper = 1.0 + take_peak(2)
 
-    centre = 0.625 * upper
-    half_span = 0.375 * upper
-    spread_ratio = 5.0 / 3.0
-    weight_prev = 0.6
-    zero = jnp.zeros_like(upper)
-    delta = [1.0 / centre, zero, zero]
-    sigma = list(delta)
-    rho = [zero + 1.0, zero, zero, zero]
-
-    def apply(rho, delta):
-        rho = list(rho)
-        for j in range(3):
-            rho[j] = rho[j] - delta[j]
-            rho[j + 1] = rho[j + 1] + delta[j]
-        return rho
-
-    for _ in range(SWEEPS):
-        rho = apply(rho, delta)
-        weight = 1.0 / (2.0 * spread_ratio - weight_prev)
-        gain = 2.0 * weight / half_span
-        delta = [weight * weight_prev * delta[j] + gain * rho[j] for j in range(3)]
-        sigma = [sigma[j] + delta[j] for j in range(3)]
-        weight_prev = weight
-    rho = apply(rho, delta)
-
-    parts = []
-    for b in range(NB):
-        residual = rho[0] * loads_v[b] + rho[1] * ksum[0, b] + rho[2] * ksum[1, b] + rho[3] * ksum[2, b]
-        res_v[b] = residual
-        parts.append(split(residual))
-    pair = dot(jnp.concatenate(parts, axis=1), oh[...], NT)
-    part = pair[:VEC] + pair[VEC:]
-
-    for j, piece in enumerate(regroup([part[8 * i:8 * i + 8] for i in range(3)], NX, 32)):
-        i_s[j] = piece
+    scale = (8.0 / 3.0) / upper
+    start = 5.0 / 3.0 - scale
+    square = start * start
+    final = 4.0 * (5.0 / 3.0) ** 3 - 3.0 * (5.0 / 3.0)
+    rho = [start * (4.0 * square - 3.0) * (1.0 / final), (12.0 * square - 3.0) * scale * (1.0 / final),
+           start * (scale * scale) * (12.0 / final), scale * (scale * scale) * (4.0 / final)]
+    sigma = [rho[1] + (rho[2] + rho[3]), rho[2] + rho[3], rho[3]]
+
+    for j in range(NX):
+        i_s[j] = rho[0] * shares[0][j] + rho[1] * shares[1][j] + (rho[2] * shares[2][j] + rho[3] * shares[3][j])
     side = NX * zh + x
     i_r[zl, side] = i_s[x]
     plane = [(dx, dz) for dx in range(NX) for dz in range(NZ) if dx or dz]
@@ -336,15 +322,15 @@
         pending.append(i_copy(dx, dz).wait_send)
 
     for b in range(NB):
+        res_v[b] = rho[0] * loads_v[b] + rho[1] * ksum[0, b] + rho[2] * ksum[1, b] + rho[3] * ksum[2, b]
         corr_v[b] = sigma[0] * own[0, b] + sigma[1] * own[1, b] + sigma[2] * own[2, b]
     for d in range(1, NG):
         inv_copy(d).wait_recv()
     for i in range(NY):
         block = jnp.concatenate([inv_r[j, i] for j in range(NG)], axis=0).T
         high = block.astype(BF16)
-        rows = slice(i * BS, (i + 1) * BS)
-        wc[rows, 0:BS] = high
-        wc[rows, BS:2 * BS] = (block - high.astype(F32)).astype(BF16)
+        wc[i, :, 0:BS] = high
+        wc[i, :, BS:2 * BS] = (block - high.astype(F32)).astype(BF16)
 
     for dx, dz in reversed(plane):
         i_arrival(dx, dz).wait_recv()
@@ -366,10 +352,16 @@
     for d in (4, 3, 5, 2, 6, 1, 7):
         c_copy(d).start()
         pending.append(c_copy(d).wait_send)
-    for d in (1, 7, 2, 6, 3, 5, 4):
-        c_arrival(d).wait_recv()
-    fields = jnp.concatenate([split(c_r[i]) for i in range(NY)], axis=1)
-    coarse = folded(dot(fields, wc[...], NN))
+    full = None
+    for pair in ((0, 1), (7, 2), (6, 3), (5, 4)):
+        for d in pair:
+            if d:
+                c_arrival(d).wait_recv()
+        for d in pair:
+            came = mod(y - d + NY, NY)
+            term = dot(split(c_r[came]), wc[came], NN)
+            full = term if full is None else full + term
+    coarse = folded(full)
 
     low = lax.broadcasted_iota(jnp.int32, (8, BS), 1) < 64
     t0, t1, t2 = coarse[0:8], coarse[8:16], coarse[16:24]
@@ -455,7 +447,7 @@
             pltpu.VMEM((3, 8, 8, BS), F32),
             pltpu.VMEM((NG, NY, ROWS, BS), F32),
             pltpu.VMEM((NG, NY, ROWS, BS), F32),
-            pltpu.VMEM((NY * BS, 2 * BS), BF16),
+            pltpu.VMEM((NY, BS, 2 * BS), BF16),
             pltpu.VMEM((BS, NB * BS), BF16),
             pltpu.VMEM((BS, NB * BS), BF16),
             pltpu.VMEM((NX, 8, BS), F32),

time: 50 us -> 49.6 us (level)
  no operation moved by 1% of the time
where the time goes in v4:
time: 49.6 us; the launch traced here: 49.5 us
  Pallas kernels  48.9 us (99%)
  between operations  0.64 us (1%)
    pallas_call x1, Pallas kernels, shards(): pl.pallas_call(kernel, out_shape=(pltpu.VMEM(field, F32), pltpu.VMEM(fiel...  48.2 us

profile of v4, /device:TPU:1, one launch (start us, length us, event | category | flops | bytes accessed | tf_op | source)
XLA Modules:
  0.0 49.5 jit_solution(4855396310463820020)
XLA Ops:
  0.6 48.2 %shard_map.95 = (f32[4,24,128]{2,1,0:T(8,128)S(1)}, f32[4,24,128]{2,1,0:T(8,128)S(1)}) custom-call(s32[4,4]{1,0:T(4,128)} %nbr_h.1, s32[4,4]{1,0:T(4,128)} %msk_h.1, s32[4]{0:T(128)} %snd_h.1, f32[4,24,128]{2,1,0:T(8,128)} %loads_h.1, f32[4,128]{1,0:T(4,128)} %diag_h.1, f32[4,4,128,128]{3,2,1,0:T(8,128)} %stiff_h.1, s32[4,128]{1,0:T(4,128)} %agg_h.1, ...), custom_call_target="tpu_custom_call" | custom-call | tf_op jit(solution)/shard_map/pallas_call | solution.py:427
  48.9 0.7 %shard_map.96 = (f32[4,24,128]{2,1,0:T(8,128)}, f32[4,24,128]{2,1,0:T(8,128)}) custom-call(f32[4,24,128]{2,1,0:T(8,128)S(1)} %get-tuple-element.4.corr_v, f32[4,24,128]{2,1,0:T(8,128)S(1)} %get-tuple-element.5.res_v), custom_call_target="tpu_custom_call" | custom-call | tf_op jit(solution)/shard_map/pallas_call | solution.py:470

commit v5 on v4

--- a/solution.py
+++ b/solution.py
@@ -84,7 +84,7 @@
     cp_snd = pltpu.make_async_copy(snd_h, snd, lsem.at[8])
     cp_msk = pltpu.make_async_copy(msk_h, msk, lsem.at[9])
     cp_nbr = pltpu.make_async_copy(nbr_h, nbr, lsem.at[10])
-    for cp in [cp_loads, cp_diag, cp_snd, cp_msk, cp_nbr] + cp_stiff + [cp_inv, cp_agg]:
+    for cp in [cp_loads, cp_diag] + cp_stiff + [cp_snd]:
         cp.start()
 
     def at(y_, zl_, core_, x_, zh_):
@@ -116,10 +116,14 @@
     right_far = jnp.logical_and(core == 1, w < N_WIDE - 1)
     pl.when(left_far)(lambda: greet((w - 1, n)))
     pl.when(right_far)(lambda: greet((w + 1, n)))
-    for d in range(1, 8):
+    for d in (4, 3, 5, 2, 6, 1, 7):
+        greet(y_peer(d))
+        greet(z_peer(d))
+    for d in (2, 6, 1, 3, 5, 7, 4):
         greet(g_peer(d))
-        greet(z_peer(d))
-        greet(y_peer(d))
+
+    for cp in (cp_msk, cp_nbr, cp_inv, cp_agg):
+        cp.start()
 
     @pl.when(w == 0)
     def _():
@@ -301,7 +305,7 @@
     side = NX * zh + x
     i_r[zl, side] = i_s[x]
     plane = [(dx, dz) for dx in range(NX) for dz in range(NZ) if dx or dz]
-    plane.sort(key=lambda p: -hops(p[0], NX) - hops(p[1], NZ))
+    plane.sort(key=lambda p: (-hops(p[1], NZ), -hops(p[0], NX)))
 
     def i_copy(dx, dz):
         other = mod(z + dz, NZ)
@@ -370,7 +374,7 @@
     d_s[1] = jnp.concatenate([jnp.where(low, u0, t1), jnp.where(low[:4], u2[0:4], t2[4:8])], axis=0)
     d_r[zh, g] = d_s[core]
     around = [(dg, dh) for dg in range(NG) for dh in range(NZH) if dg or dh]
-    around.sort(key=lambda p: -4 * p[1] - hops(p[0], NG))
+    around.sort(key=lambda p: -4 * p[1] - hops(p[0] % NX, NX))
 
     def d_copy(dg, dh):
         other = mod(g + dg, NG)

time: 49.6 us -> 49.4 us (level)
  no operation moved by 1% of the time
where the time goes in v5:
time: 49.4 us; the launch traced here: 49.3 us
  Pallas kernels  48.7 us (99%)
  between operations  0.64 us (1%)
    pallas_call x1, Pallas kernels, shards(): pl.pallas_call(kernel, out_shape=(pltpu.VMEM(field, F32), pltpu.VMEM(fiel...  48 us

profile of v5, /device:TPU:1, one launch (start us, length us, event | category | flops | bytes accessed | tf_op | source)
XLA Modules:
  0.0 49.3 jit_solution(12191227578925242320)
XLA Ops:
  0.6 48.0 %shard_map.95 = (f32[4,24,128]{2,1,0:T(8,128)S(1)}, f32[4,24,128]{2,1,0:T(8,128)S(1)}) custom-call(s32[4,4]{1,0:T(4,128)} %nbr_h.1, s32[4,4]{1,0:T(4,128)} %msk_h.1, s32[4]{0:T(128)} %snd_h.1, f32[4,24,128]{2,1,0:T(8,128)} %loads_h.1, f32[4,128]{1,0:T(4,128)} %diag_h.1, f32[4,4,128,128]{3,2,1,0:T(8,128)} %stiff_h.1, s32[4,128]{1,0:T(4,128)} %agg_h.1, ...), custom_call_target="tpu_custom_call" | custom-call | tf_op jit(solution)/shard_map/pallas_call | solution.py:431
  48.7 0.7 %shard_map.96 = (f32[4,24,128]{2,1,0:T(8,128)}, f32[4,24,128]{2,1,0:T(8,128)}) custom-call(f32[4,24,128]{2,1,0:T(8,128)S(1)} %get-tuple-element.4.corr_v, f32[4,24,128]{2,1,0:T(8,128)S(1)} %get-tuple-element.5.res_v), custom_call_target="tpu_custom_call" | custom-call | tf_op jit(solution)/shard_map/pallas_call | solution.py:474

commit v6 on v4

--- a/solution.py
+++ b/solution.py
@@ -152,9 +152,17 @@
         pending.append(lambda: pl.when(w > 0)(lambda: to_left(k).wait_send()))
         pending.append(lambda: pl.when(w < N_WIDE - 1)(lambda: to_right(k).wait_send()))
 
+    def split_ghosts(k, first):
+        for j in range(2):
+            exts[NB + first + j] = split(ghost[k, first + j])
+
     def wait_halo(k):
-        pl.when(w < N_WIDE - 1)(lambda: to_left(k).wait_recv())
-        pl.when(w > 0)(lambda: to_right(k).wait_recv())
+        pl.when(core == 0)(lambda: to_left(k).wait_recv())
+        pl.when(core == 1)(lambda: to_right(k).wait_recv())
+        split_ghosts(k, 2 - 2 * core)
+        pl.when(right_far)(lambda: to_left(k).wait_recv())
+        pl.when(left_far)(lambda: to_right(k).wait_recv())
+        split_ghosts(k, 2 * core)
 
     fill_halo(0)
 
@@ -237,8 +245,6 @@
 
     def couple(k):
         wait_halo(k)
-        for j in range(4):
-            exts[NB + j] = split(ghost[k, j])
         for b in range(NB):
             fields = jnp.concatenate([exts[nbr[b, s]] for s in range(NS)], axis=1)
             coupled = folded(dot(fields, w2[b], NN))

time: 49.6 us -> 49.6 us (level)
  no operation moved by 1% of the time
where the time goes in v6:
time: 49.6 us; the launch traced here: 49.5 us
  Pallas kernels  48.9 us (99%)
  between operations  0.64 us (1%)
    pallas_call x1, Pallas kernels, shards(): pl.pallas_call(kernel, out_shape=(pltpu.VMEM(field, F32), pltpu.VMEM(fiel...  48.2 us

profile of v6, /device:TPU:1, one launch (start us, length us, event | category | flops | bytes accessed | tf_op | source)
XLA Modules:
  0.0 49.5 jit_solution(1554511458315488646)
XLA Ops:
  0.6 48.2 %shard_map.95 = (f32[4,24,128]{2,1,0:T(8,128)S(1)}, f32[4,24,128]{2,1,0:T(8,128)S(1)}) custom-call(s32[4,4]{1,0:T(4,128)} %nbr_h.1, s32[4,4]{1,0:T(4,128)} %msk_h.1, s32[4]{0:T(128)} %snd_h.1, f32[4,24,128]{2,1,0:T(8,128)} %loads_h.1, f32[4,128]{1,0:T(4,128)} %diag_h.1, f32[4,4,128,128]{3,2,1,0:T(8,128)} %stiff_h.1, s32[4,128]{1,0:T(4,128)} %agg_h.1, ...), custom_call_target="tpu_custom_call" | custom-call | tf_op jit(solution)/shard_map/pallas_call | solution.py:433
  48.9 0.7 %shard_map.96 = (f32[4,24,128]{2,1,0:T(8,128)}, f32[4,24,128]{2,1,0:T(8,128)}) custom-call(f32[4,24,128]{2,1,0:T(8,128)S(1)} %get-tuple-element.4.corr_v, f32[4,24,128]{2,1,0:T(8,128)S(1)} %get-tuple-element.5.res_v), custom_call_target="tpu_custom_call" | custom-call | tf_op jit(solution)/shard_map/pallas_call | solution.py:476
